TPU v7x, 32 devices: a whole 2x2x4 slice. The times are simulated.
32 devices in a mesh: nodes: 16 (over z, y, x), rep: 2 (over core).
Axes of the slice: x: 2, y: 2, z: 4, core: 2. Of those that a mesh axis runs over, the one named last changes fastest.
Arguments:
- node_latent: bfloat16 [5120, 512], P(('nodes', 'rep')), may hold values from -6 to 6
- edge_saved: bfloat16 [40960, 512], P(('nodes', 'rep')), may hold values from -6 to 6
- node_cot: bfloat16 [5120, 512], P(('nodes', 'rep')), may hold values from -6 to 6
- edge_cot: bfloat16 [40960, 512], P(('nodes', 'rep')), may hold values from -6 to 6
- senders: int32 [40960], P(('nodes', 'rep')), may hold values from 0 to 447, as said below
- receivers: int32 [40960], P(('nodes', 'rep')), may hold values from 0 to 319
- ghost_rows: int32 [16, 16, 8], P('nodes'), may hold values from 0 to 319, as said below
- w_edge_in: bfloat16 [1536, 512], replicated, may hold values from -0.15625 to 0.15625
- w_edge_out: bfloat16 [512, 512], replicated, may hold values from -0.25 to 0.25
- edge_gain: float32 [512], replicated, may hold values from 0.5 to 2
- edge_offset: float32 [512], replicated, may hold values from -3 to 3
- w_node_in: bfloat16 [1024, 512], replicated, may hold values from -0.1875 to 0.1875
- w_node_out: bfloat16 [512, 512], replicated, may hold values from -0.25 to 0.25
- node_gain: float32 [512], replicated, may hold values from 0.5 to 2
Outputs:
- grad_nodes: bfloat16 [5120, 512], P(('nodes', 'rep'))
- grad_edges: bfloat16 [40960, 512], P(('nodes', 'rep'))
- grad_edge_in: bfloat16 [1536, 512], replicated
- grad_edge_out: bfloat16 [512, 512], replicated
- grad_node_in: bfloat16 [1024, 512], replicated
- grad_node_out: bfloat16 [512, 512], replicated
Inputs may be any that keep to these rules, and one draw needn't show every extreme that they name: `senders`: A sender below 320 is a node of the edge's own partition; otherwise it is 320 + q * 8 + s, the ghost slot s of the list of a partition q other than the edge's own. Each list ghost_rows[q, p] holds 8 distinct rows.
All inputs are finite; a program needn't handle non-finite values.
Results may differ from a plain program's by a relative error of at most 0.008.
Values may be sent and summed in bfloat16 or wider, within the bound.
A program may use at most 128 MiB of HBM per device.

v0:
```python
import math
import jax
import jax.numpy as jnp
from jax import lax
from jax.sharding import PartitionSpec as P

EPS = 1e-05


def swapped(array, axis, bit):
    return lax.ppermute(array, axis, [(i, i ^ 1 << bit) for i in range(lax.axis_size(axis))])


def mat_mul(left, right):
    return jnp.dot(left, right, preferred_element_type=jnp.float32)


def mat_tn(left, right):
    return lax.dot_general(
        left, right, (((0,), (0,)), ((), ())), preferred_element_type=jnp.float32
    )


def mat_nt(left, right):
    return lax.dot_general(
        left, right, (((1,), (1,)), ((), ())), preferred_element_type=jnp.float32
    )


def silu_slope(value):
    sigmoid_v = jax.nn.sigmoid(value)
    return sigmoid_v * (1.0 + value * (1.0 - sigmoid_v))


def norm_forward(value):
    centred = value - jnp.mean(value, axis=-1, keepdims=True)
    inverse = lax.rsqrt(jnp.mean(centred * centred, axis=-1, keepdims=True) + EPS)
    return (centred * inverse, inverse)


def norm_backward(grad_hat, normed, inverse):
    return inverse * (
        grad_hat
        - jnp.mean(grad_hat, axis=-1, keepdims=True)
        - normed * jnp.mean(grad_hat * normed, axis=-1, keepdims=True)
    )


def edge_forward(edge_block, send_rows, recv_rows, w_edge_in, w_edge_out, edge_gain, edge_offset):
    latent_width = edge_block.shape[1]
    pre_act = (
        mat_mul(edge_block, w_edge_in[:latent_width])
        + mat_mul(send_rows, w_edge_in[latent_width : 2 * latent_width])
        + mat_mul(recv_rows, w_edge_in[2 * latent_width :])
    )
    edge_hidden = jax.nn.silu(pre_act).astype(jnp.bfloat16)
    edge_normed, edge_inverse = norm_forward(mat_mul(edge_hidden, w_edge_out))
    message = edge_normed * edge_gain + edge_offset
    return (pre_act, edge_hidden, edge_normed, edge_inverse, message)


def edge_backward(
    edge_block,
    send_rows,
    recv_rows,
    edge_cot,
    message_grad,
    saved,
    w_edge_in,
    w_edge_out,
    edge_gain,
):
    pre_act, edge_hidden, edge_normed, edge_inverse = saved
    latent_width = edge_block.shape[1]
    grad_out = norm_backward(message_grad * edge_gain, edge_normed, edge_inverse).astype(
        jnp.bfloat16
    )
    grad_act = (mat_nt(grad_out, w_edge_out) * silu_slope(pre_act)).astype(jnp.bfloat16)
    in_grad = jnp.concatenate(
        [mat_tn(edge_block, grad_act), mat_tn(send_rows, grad_act), mat_tn(recv_rows, grad_act)], 0
    )
    out_grad = mat_tn(edge_hidden, grad_out)
    edge_grad = (edge_cot.astype(jnp.float32) + mat_nt(grad_act, w_edge_in[:latent_width])).astype(
        jnp.bfloat16
    )
    send_grad = mat_nt(grad_act, w_edge_in[latent_width : 2 * latent_width])
    recv_grad = mat_nt(grad_act, w_edge_in[2 * latent_width :])
    return (edge_grad, send_grad, recv_grad, in_grad, out_grad)


def node_pass(node_rows, totals_b, node_cot, w_node_in, w_node_out, node_gain):
    latent_width = node_rows.shape[1]
    node_pre = mat_mul(node_rows, w_node_in[:latent_width]) + mat_mul(
        totals_b, w_node_in[latent_width:]
    )
    node_hidden = jax.nn.silu(node_pre).astype(jnp.bfloat16)
    node_normed, node_inverse = norm_forward(mat_mul(node_hidden, w_node_out))
    grad_out = norm_backward(
        node_cot.astype(jnp.float32) * node_gain, node_normed, node_inverse
    ).astype(jnp.bfloat16)
    grad_act = (mat_nt(grad_out, w_node_out) * silu_slope(node_pre)).astype(jnp.bfloat16)
    in_grad = jnp.concatenate([mat_tn(node_rows, grad_act), mat_tn(totals_b, grad_act)], 0)
    direct_grad = mat_nt(grad_act, w_node_in[:latent_width])
    totals_grad = mat_nt(grad_act, w_node_in[latent_width:]).astype(jnp.bfloat16)
    return (direct_grad, totals_grad, in_grad, mat_tn(node_hidden, grad_out))


def shards(
    node_latent,
    edge_saved,
    node_cot,
    edge_cot,
    senders,
    receivers,
    ghost_rows,
    w_edge_in,
    w_edge_out,
    edge_gain,
    edge_offset,
    w_node_in,
    w_node_out,
    node_gain,
):
    latent_width = node_latent.shape[1]
    edge_latent = swapped(edge_saved, "rep", 0)
    partition = lax.all_gather(node_latent, "rep", axis=0, tiled=True)
    part_rows = partition.shape[0]
    ghost_lists = ghost_rows[0]
    part_count = ghost_lists.shape[0]
    slot_count = ghost_lists.shape[1]
    outgoing = partition[ghost_lists.reshape(-1)].reshape(part_count, slot_count, latent_width)
    ghosts = lax.all_to_all(outgoing, "nodes", split_axis=0, concat_axis=0, tiled=True)
    node_table = jnp.concatenate(
        [partition, ghosts.reshape(part_count * slot_count, latent_width)], 0
    )
    send_rows = node_table[senders]
    recv_rows = partition[receivers]
    pre_act, edge_hidden, edge_normed, edge_inverse, message = edge_forward(
        edge_latent, send_rows, recv_rows, w_edge_in, w_edge_out, edge_gain, edge_offset
    )
    partial_totals = jax.ops.segment_sum(message, receivers, num_segments=part_rows)
    totals = lax.psum_scatter(partial_totals, "rep", scatter_dimension=0, tiled=True)
    direct_grad, totals_grad, node_in_grad, node_out_grad = node_pass(
        node_latent, totals.astype(jnp.bfloat16), node_cot, w_node_in, w_node_out, node_gain
    )
    partition_totals_grad = lax.all_gather(totals_grad, "rep", axis=0, tiled=True)
    message_grad = edge_cot.astype(jnp.float32) + partition_totals_grad[receivers].astype(
        jnp.float32
    )
    edge_grad, send_grad, recv_grad, edge_in_grad, edge_out_grad = edge_backward(
        edge_latent,
        send_rows,
        recv_rows,
        edge_cot,
        message_grad,
        (pre_act, edge_hidden, edge_normed, edge_inverse),
        w_edge_in,
        w_edge_out,
        edge_gain,
    )
    table_grad = jax.ops.segment_sum(send_grad, senders, num_segments=node_table.shape[0])
    row_grad = table_grad[:part_rows] + jax.ops.segment_sum(
        recv_grad, receivers, num_segments=part_rows
    )
    ghost_grad = table_grad[part_rows:].reshape(part_count, slot_count, latent_width)
    returned = lax.all_to_all(
        ghost_grad.astype(jnp.bfloat16), "nodes", split_axis=0, concat_axis=0, tiled=True
    ).astype(ghost_grad.dtype)
    row_grad = row_grad + jax.ops.segment_sum(
        returned.reshape(-1, latent_width), ghost_lists.reshape(-1), num_segments=part_rows
    )
    own_grad = lax.psum_scatter(row_grad, "rep", scatter_dimension=0, tiled=True)
    grad_nodes = (own_grad + direct_grad + node_cot.astype(jnp.float32)).astype(jnp.bfloat16)
    weight_grads = (edge_in_grad, edge_out_grad, node_in_grad, node_out_grad)
    device_count = lax.axis_size("nodes") * lax.axis_size("rep")
    edge_scale = 1.0 / math.sqrt(senders.shape[0] * device_count)
    node_scale = 1.0 / math.sqrt(node_latent.shape[0] * device_count)
    weight_total = lax.psum(
        (weight_grads[0], weight_grads[1], weight_grads[2], weight_grads[3]), ("nodes", "rep")
    )
    return (
        grad_nodes,
        edge_grad,
        (weight_total[0] * edge_scale).astype(jnp.bfloat16),
        (weight_total[1] * edge_scale).astype(jnp.bfloat16),
        (weight_total[2] * node_scale).astype(jnp.bfloat16),
        (weight_total[3] * node_scale).astype(jnp.bfloat16),
    )


def solution(mesh):
    return jax.shard_map(
        shards,
        mesh=mesh,
        in_specs=(
            P(("nodes", "rep"), None),
            P(("nodes", "rep"), None),
            P(("nodes", "rep"), None),
            P(("nodes", "rep"), None),
            P(("nodes", "rep")),
            P(("nodes", "rep")),
            P("nodes", None, None),
            P(),
            P(),
            P(),
            P(),
            P(),
            P(),
            P(),
        ),
        out_specs=(P(("nodes", "rep"), None), P(("nodes", "rep"), None), P(), P(), P(), P()),
        check_vma=False,
    )
```

profile of v0, /device:TPU:0, one launch (start us, length us, event | category | flops | bytes accessed | tf_op | source)
XLA Modules:
  0.0 329.2 jit_solution(6399339282677917739)
XLA Ops:
  7.2 2.5 all_gather.6
  12.1 8.2 %all-to-all-start = ((bf16[16,8,512]{2,1,0:T(8,128)(2,1)}), bf16[16,8,512]{2,1,0:T(8,128)(2,1)S(1)}, u32[]{:S(2)}, u32[]{:S(2)}) async-start(bf16[16,8,512]{2,1,0:T(8,128)(2,1)} %bitcast.1), calls=%async_computation | async-start | bytes 262144 | tf_op jit(solution)/shard_map/all_to_all | solution.py:132
  21.1 4.1 %gather_fusion.2 = bf16[1280,512]{1,0:T(8,128)(2,1)S(1)} fusion(bf16[320,512]{1,0:T(8,128)(2,1)S(1)} %all_gather.6, s32[2048]{0:T(1024)S(1)} %pad_clamp_fusion), kind=kCustom, calls=%fused_computation.2 | custom fusion | bytes 2626560 | tf_op jit(solution)/shard_map/gather | solution.py:137
  25.3 3.8 %fusion.15 = f32[1280,512]{1,0:T(8,128)} fusion(bf16[1280,512]{1,0:T(8,128)(2,1)S(1)} %gather_fusion.2, bf16[1536,512]{1,0:T(8,128)(2,1)} %param.21), kind=kOutput, calls=%fused_computation.46 | convolution fusion | flops 671088640 | bytes 4456448 | tf_op jit(solution)/shard_map/dot_general | solution.py:15
  29.1 4.1 %gather_fusion.1 = bf16[1280,512]{1,0:T(8,128)(2,1)S(1)} fusion(bf16[448,512]{1,0:T(8,128)(2,1)S(1)} %pad_maximum_fusion.2, s32[2048]{0:T(1024)S(1)} %pad_clamp_fusion.1), kind=kCustom, calls=%fused_computation.1 | custom fusion | bytes 2626560 | tf_op jit(solution)/shard_map/gather | solution.py:136
  33.2 2.4 fusion.19
  35.7 4.2 %multiply_convert_fusion.2 = (bf16[1280,512]{1,0:T(8,128)(2,1)S(1)}, f32[1280,512]{1,0:T(8,128)}) fusion(f32[1280,512]{1,0:T(8,128)S(1)} %copy-done.12, f32[1280,512]{1,0:T(8,128)S(1)} %fusion.19, bf16[1280,512]{1,0:T(8,128)(2,1)} %collective-permute-done, bf16[1536,512]{1,0:T(8,128)(2,1)} %param.21), kind=kOutput, calls=%fused_computation.22 | convolution fusion | flops 675676160 | bytes 11010048 | tf_op jit(solution)/shard_map/dot_general | solution.py:15
  41.7 1.9 multiply_add_fusion
  43.6 3.2 copy.28
  46.9 11.1 %scatter_custom_fusion = f32[320,512]{1,0:T(8,128)} fusion(s32[1280]{0:T(1024)S(1)} %copy-done.34, f32[1280,512]{1,0:T(8,128)} %copy.28, f32[]{:T(128)} %constant.10.clone.1), kind=kCustom, calls=%fused_computation.70 | custom fusion | flops 655360 | bytes 655872 | tf_op jit(solution)/shard_map/scatter-add | solution.py:141
  58.1 2.4 copy.27
  60.5 2.0 fusion.11
  62.5 5.1 %reduce-scatter.3.cloned.1.call-done = f32[160,512]{1,0:T(8,128)} async-done(((f32[320,512]{1,0:T(8,128)}), f32[160,512]{1,0:T(8,128)}) %reduce-scatter.3.cloned.1.call-update) | async-done | bytes 327696 | tf_op jit(solution)/shard_map/reduce_scatter | solution.py:142
  72.7 2.2 all_gather.7
  74.9 4.7 %gather_fusion.3 = bf16[1280,512]{1,0:T(8,128)(2,1)} fusion(bf16[320,512]{1,0:T(8,128)(2,1)S(1)} %all_gather.7, s32[2048]{0:T(1024)S(1)} %pad_clamp_fusion), kind=kCustom, calls=%fused_computation.3 | custom fusion | bytes 2626560 | tf_op jit(solution)/shard_map/gather | solution.py:147
  79.6 2.4 copy.29
  82.1 2.7 fusion.4
  88.0 2.4 fusion.17
  90.5 2.4 fusion.13
  92.8 10.6 %scatter_custom_fusion.1 = f32[448,512]{1,0:T(8,128)S(1)} fusion(s32[1280]{0:T(1024)S(1)} %copy-done.36, f32[1280,512]{1,0:T(8,128)} %fusion.17, f32[]{:T(128)} %constant.10.clone.1), kind=kCustom, calls=%fused_computation.55 | custom fusion | flops 655360 | bytes 918016 | tf_op jit(solution)/shard_map/scatter-add | solution.py:161
  104.1 3.2 fusion.50
  108.8 6.7 %all-to-all-start.1 = ((bf16[16,8,512]{2,1,0:T(8,128)(2,1)}), bf16[16,8,512]{2,1,0:T(8,128)(2,1)S(1)}, u32[]{:S(2)}, u32[]{:S(2)}) async-start(bf16[16,8,512]{2,1,0:T(8,128)(2,1)} %fusion.37), calls=%async_computation.2 | async-start | bytes 262144 | tf_op jit(solution)/shard_map/all_to_all | solution.py:166
  115.7 10.7 %scatter_fusion = f32[320,512]{1,0:T(8,128)S(1)} fusion(f32[320,512]{1,0:T(8,128)S(1)} %slice.42, s32[1280]{0:T(1024)S(1)} %copy-done.34, f32[1280,512]{1,0:T(8,128)} %fusion.13), kind=kCustom, calls=%fused_computation.6 | custom fusion | flops 655360 | bytes 7869440 | tf_op jit(solution)/shard_map/scatter-add | solution.py:162
  131.7 3.2 pad_maximum_fusion.1
  136.6 1.9 fusion.51
  138.5 2.3 convolution_bitcast_fusion
  140.8 2.0 pad_maximum_fusion
  144.1 3.0 fusion.1
  147.1 2.5 copy.32
  149.6 2.0 fusion.7
  151.6 164.3 %all-reduce.3.cloned.1.call-done = (f32[1536,512]{1,0:T(8,128)}, f32[512,512]{1,0:T(8,128)}, f32[1024,512]{1,0:T(8,128)}, f32[512,512]{1,0:T(8,128)}) async-done(((f32[1536,512]{1,0:T(8,128)}, f32[512,512]{1,0:T(8,128)}, f32[1024,512]{1,0:T(8,128)}, f32[512,512]{1,0:T(8,128)}), (f32[1536,512]{1,0:T(8,128)}, f32[512,512]{1,0:T(8,128)}, f32[1024,512]{1,0:T(8,128)}, ...) | async-done | bytes 7340048 | tf_op jit(solution)/shard_map/psum | solution.py:178
  315.9 3.6 %multiply_convert_fusion = bf16[1536,512]{1,0:T(8,128)(2,1)} fusion(f32[1536,512]{1,0:T(8,128)} %get-tuple-element.22), kind=kLoop, calls=%fused_computation.14 | loop fusion | flops 1572864 | bytes 4718592 | tf_op jit(solution)/shard_map/convert_element_type | solution.py:184
  (132 shorter events, 27.0 us)
Async XLA Ops:
  7.2 32.7 %copy-start = (bf16[512,512]{1,0:T(8,128)(2,1)S(1)}, bf16[512,512]{1,0:T(8,128)(2,1)}, u32[]{:S(2)}) copy-start(bf16[512,512]{1,0:T(8,128)(2,1)} %param.22) | copy-start | bytes 1572868
  12.1 17.0 %all-to-all-start = ((bf16[16,8,512]{2,1,0:T(8,128)(2,1)}), bf16[16,8,512]{2,1,0:T(8,128)(2,1)S(1)}, u32[]{:S(2)}, u32[]{:S(2)}) async-start(bf16[16,8,512]{2,1,0:T(8,128)(2,1)} %bitcast.1), calls=%async_computation | async-start | bytes 262144 | tf_op jit(solution)/shard_map/all_to_all | solution.py:132
  20.3 47.3 %reduce-scatter.3.cloned.1.call-start = ((), (), s32[]{:S(2)}) async-start(), calls=%async_computation.4 | async-start | bytes 983040 | tf_op jit(solution)/shard_map/reduce_scatter | solution.py:142
  20.3 15.3 %collective-permute-start = (bf16[1280,512]{1,0:T(8,128)(2,1)}, bf16[1280,512]{1,0:T(8,128)(2,1)}, u32[]{:S(2)}, u32[]{:S(2)}) collective-permute-start(bf16[1280,512]{1,0:T(8,128)(2,1)} %param.15), channel_id=1, source_target_pairs={{0,1},{1,0},{2,3},{3,2},{4,5},{5,4},{6,7},{7,6},{8,9},{9,8},{10,11... | collective-permute-start | bytes 3932168 | tf_op jit(solution)/shard_map/ppermute | solution.py:11
  21.1 4.1 %copy-start.36 = (s32[1280]{0:T(1024)S(1)}, s32[1280]{0:T(1024)}, u32[]{:S(2)}) copy-start(s32[1280]{0:T(1024)} %param.18) | copy-start | bytes 15364
  25.3 3.8 %copy-start.7 = (bf16[1280,512]{1,0:T(8,128)(2,1)}, bf16[1280,512]{1,0:T(8,128)(2,1)S(1)}, u32[]{:S(2)}) copy-start(bf16[1280,512]{1,0:T(8,128)(2,1)S(1)} %gather_fusion.2) | copy-start | bytes 3932164
  33.2 2.4 copy-start.5
  33.2 2.4 copy-start.12
  43.6 3.2 copy-start.34
  46.8 13.6 %copy-start.16 = (bf16[160,512]{1,0:T(8,128)(2,1)S(1)}, bf16[160,512]{1,0:T(8,128)(2,1)}, u32[]{:S(2)}) copy-start(bf16[160,512]{1,0:T(8,128)(2,1)} %param.14) | copy-start | bytes 491524
  62.5 8.4 %copy-start.30 = (bf16[160,512]{1,0:T(8,128)(2,1)S(1)}, bf16[160,512]{1,0:T(8,128)(2,1)}, u32[]{:S(2)}) copy-start(bf16[160,512]{1,0:T(8,128)(2,1)} %param.16) | copy-start | bytes 491524
  62.5 8.4 %copy-start.38 = (f32[512]{0:T(512)S(1)}, f32[512]{0:T(512)}, u32[]{:S(2)}) copy-start(f32[512]{0:T(512)} %param.27) | copy-start | bytes 6148
  67.6 3.6 %copy-start.39 = (bf16[512,512]{1,0:T(8,128)(2,1)S(1)}, bf16[512,512]{1,0:T(8,128)(2,1)}, u32[]{:S(2)}) copy-start(bf16[512,512]{1,0:T(8,128)(2,1)} %param.26) | copy-start | bytes 1572868
  69.1 2.4 copy-start.32
  82.0 2.7 copy-start.2
  82.0 2.7 copy-start.4
  88.0 2.4 copy-start.9
  92.8 11.3 %copy-start.8 = (bf16[1280,512]{1,0:T(8,128)(2,1)S(1)}, bf16[1280,512]{1,0:T(8,128)(2,1)}, u32[]{:S(2)}) copy-start(bf16[1280,512]{1,0:T(8,128)(2,1)} %copy-done.7) | copy-start | bytes 3932164
  104.1 3.2 copy-start.21
  104.1 3.2 copy-start.31
  104.1 3.2 copy-start.33
  108.8 20.3 %all-to-all-start.1 = ((bf16[16,8,512]{2,1,0:T(8,128)(2,1)}), bf16[16,8,512]{2,1,0:T(8,128)(2,1)S(1)}, u32[]{:S(2)}, u32[]{:S(2)}) async-start(bf16[16,8,512]{2,1,0:T(8,128)(2,1)} %fusion.37), calls=%async_computation.2 | async-start | bytes 262144 | tf_op jit(solution)/shard_map/all_to_all | solution.py:166
  115.6 10.8 %copy-start.19 = (bf16[160,512]{1,0:T(8,128)(2,1)S(1)}, bf16[160,512]{1,0:T(8,128)(2,1)}, u32[]{:S(2)}) copy-start(bf16[160,512]{1,0:T(8,128)(2,1)} %copy-done.18) | copy-start | bytes 491524
  115.6 10.8 %copy-start.26 = (f32[160,512]{1,0:T(8,128)S(1)}, f32[160,512]{1,0:T(8,128)}, u32[]{:S(2)}) copy-start(f32[160,512]{1,0:T(8,128)} %reduce-scatter.3.cloned.1.call-done) | copy-start | bytes 983044
  115.6 12.2 %copy-start.17 = (bf16[160,512]{1,0:T(8,128)(2,1)S(1)}, bf16[160,512]{1,0:T(8,128)(2,1)}, u32[]{:S(2)}) copy-start(bf16[160,512]{1,0:T(8,128)(2,1)} %param.14) | copy-start | bytes 491524
  115.6 34.0 %reduce-scatter.5.cloned.1.call-start = ((), (), s32[]{:S(2)}) async-start(), calls=%async_computation.5 | async-start | bytes 983040 | tf_op jit(solution)/shard_map/reduce_scatter | solution.py:172
  131.6 3.3 %copy-start.6 = (bf16[1280,512]{1,0:T(8,128)(2,1)S(1)}, bf16[1280,512]{1,0:T(8,128)(2,1)}, u32[]{:S(2)}) copy-start(bf16[1280,512]{1,0:T(8,128)(2,1)} %copy-done.5) | copy-start | bytes 3932164
  131.6 3.3 copy-start.10
  131.6 184.3 %all-reduce.3.cloned.1.call-start = ((), (), s32[]{:S(2)}) async-start(), calls=%async_computation.6 | async-start | bytes 14680064 | tf_op jit(solution)/shard_map/psum | solution.py:178
  147.1 2.5 copy-start.14
  315.9 3.6 %copy-start.28 = (f32[512,512]{1,0:T(8,128)S(1)}, f32[512,512]{1,0:T(8,128)}, u32[]{:S(2)}) copy-start(f32[512,512]{1,0:T(8,128)} %get-tuple-element.23) | copy-start | bytes 3145732
  315.9 4.6 %copy-start.15 = (f32[1024,512]{1,0:T(8,128)S(1)}, f32[1024,512]{1,0:T(8,128)}, u32[]{:S(2)}) copy-start(f32[1024,512]{1,0:T(8,128)} %get-tuple-element.24) | copy-start | bytes 6291460
  (15 other events, 22.7 us)
Sparse Core Ops, SparseCore 0:
  58.1 9.4 reduce-scatter.2
  131.7 9.3 reduce-scatter.4
  147.3 168.5 all-reduce.2
where the time goes:
time: 330 us; the launch traced here: 329 us
  waiting for transfers between devices  169 us (51%)
  other arithmetic  53.9 us (16%)
  matrix products  40.7 us (12%)
  local copies, waits for them, and re-layouts  31 us (9%)
  starting transfers between devices  15.1 us (5%)
  between operations  14.3 us (4%)
  blocking collectives  4.72 us (1%)
    psum x1, waiting for transfers between devices, shards(): lax.psum((weight_grads[0], weight_grads[1], weight_grads[2], weight_grads...  164 us
    dot_general x7, matrix products, mat_mul(): return jnp.dot(left, right, preferred_element_type=jnp.float32)  16.4 us
    dot_general x7, matrix products, mat_tn(): lax.dot_general(left, right, (((0,), (0,)), ((), ())), preferred_element_...  12.4 us
    dot_general x7, matrix products, mat_nt(): lax.dot_general(left, right, (((1,), (1,)), ((), ())), preferred_element_...  11.9 us
    scatter-add x1, other arithmetic, shards(): jax.ops.segment_sum(message, receivers, num_segments=part_rows)  11.1 us
    scatter-add x1, other arithmetic, shards(): jax.ops.segment_sum(recv_grad, receivers, num_segments=part_rows)  10.7 us
    scatter-add x1, other arithmetic, shards(): jax.ops.segment_sum(send_grad, senders, num_segments=node_table.shape[0])  10.6 us
    unnamed x85, local copies, waits for them, and re-layouts  10.1 us
  transfers between devices with their start and end apart: 6, of which 2 were waited for; matrix products, arithmetic and copies ran while one was open for 15% of the time, Pallas kernels for 0%

commit v1 on v0

--- a/solution.py
+++ b/solution.py
@@ -176,7 +176,10 @@
     edge_scale = 1.0 / math.sqrt(senders.shape[0] * device_count)
     node_scale = 1.0 / math.sqrt(node_latent.shape[0] * device_count)
     weight_total = lax.psum(
-        (weight_grads[0], weight_grads[1], weight_grads[2], weight_grads[3]), ("nodes", "rep")
+        lax.psum(
+            (weight_grads[0], weight_grads[1], weight_grads[2], weight_grads[3]), axis_name="rep"
+        ),
+        axis_name="nodes",
     )
     return (
         grad_nodes,

time: 330 us -> 406 us (1.23)
  waiting for transfers between devices: 169 us -> 246 us
    psum x0 -> x1, waiting for transfers between devices: none -> 238 us  [shards(): lax.psum(lax.psum((weight_grads[0], weight_grads[1], weight_grads[2], wei...]
    psum x1, waiting for transfers between devices: 164 us -> 0.02 us  [shards(): lax.psum((weight_grads[0], weight_grads[1], weight_grads[2], weight_grads...]
    dot_general x7, matrix products: 12.4 us -> 7.91 us  [mat_tn(): lax.dot_general(left, right, (((0,), (0,)), ((), ())), preferred_element_...]
    unnamed x85 -> x73, local copies, waits for them, and re-layouts: 10.1 us -> 9.69 us
  transfers between devices with their start and end apart: 6 -> 7, of which waited for: 2 -> 3; matrix products, arithmetic and copies ran while one was open for 15% -> 15% of each run, Pallas kernels for 0% -> 0%
where the time goes in v1:
time: 406 us; the launch traced here: 404 us
  waiting for transfers between devices  246 us (61%)
  other arithmetic  53 us (13%)
  matrix products  38.3 us (9%)
  local copies, waits for them, and re-layouts  32.8 us (8%)
  starting transfers between devices  15.2 us (4%)
  between operations  14.2 us (3%)
  blocking collectives  4.72 us (1%)
    psum x1, waiting for transfers between devices, shards(): lax.psum(lax.psum((weight_grads[0], weight_grads[1], weight_grads[2], wei...  238 us
    dot_general x7, matrix products, mat_mul(): return jnp.dot(left, right, preferred_element_type=jnp.float32)  16.4 us
    dot_general x7, matrix products, mat_nt(): lax.dot_general(left, right, (((1,), (1,)), ((), ())), preferred_element_...  14 us
    scatter-add x1, other arithmetic, shards(): jax.ops.segment_sum(send_grad, senders, num_segments=node_table.shape[0])  11.4 us
    scatter-add x1, other arithmetic, shards(): jax.ops.segment_sum(message, receivers, num_segments=part_rows)  11.1 us
    scatter-add x1, other arithmetic, shards(): jax.ops.segment_sum(recv_grad, receivers, num_segments=part_rows)  10.6 us
    unnamed x73, local copies, waits for them, and re-layouts  9.69 us
    all_to_all x1, starting transfers between devices, shards(): lax.all_to_all(outgoing, 'nodes', split_axis=0, concat_axis=0, tiled=True)  8.22 us
  transfers between devices with their start and end apart: 7, of which 3 were waited for; matrix products, arithmetic and copies ran while one was open for 15% of the time, Pallas kernels for 0%

profile of v1, /device:TPU:0, one launch (start us, length us, event | category | flops | bytes accessed | tf_op | source)
XLA Modules:
  0.0 404.4 jit_solution(8770099151280090882)
XLA Ops:
  7.2 2.5 all_gather.6
  12.1 8.2 %all-to-all-start = ((bf16[16,8,512]{2,1,0:T(8,128)(2,1)}), bf16[16,8,512]{2,1,0:T(8,128)(2,1)S(1)}, u32[]{:S(2)}, u32[]{:S(2)}) async-start(bf16[16,8,512]{2,1,0:T(8,128)(2,1)} %bitcast.1), calls=%async_computation | async-start | bytes 262144 | tf_op jit(solution)/shard_map/all_to_all | solution.py:132
  21.1 4.1 %gather_fusion.2 = bf16[1280,512]{1,0:T(8,128)(2,1)S(1)} fusion(bf16[320,512]{1,0:T(8,128)(2,1)S(1)} %all_gather.6, s32[2048]{0:T(1024)S(1)} %pad_clamp_fusion), kind=kCustom, calls=%fused_computation.2 | custom fusion | bytes 2626560 | tf_op jit(solution)/shard_map/gather | solution.py:137
  25.3 3.7 fusion.15
  29.1 4.1 %gather_fusion.1 = bf16[1280,512]{1,0:T(8,128)(2,1)S(1)} fusion(bf16[448,512]{1,0:T(8,128)(2,1)S(1)} %pad_maximum_fusion.2, s32[2048]{0:T(1024)S(1)} %pad_clamp_fusion.1), kind=kCustom, calls=%fused_computation.1 | custom fusion | bytes 2626560 | tf_op jit(solution)/shard_map/gather | solution.py:136
  33.2 2.4 fusion.19
  35.6 4.3 %multiply_convert_fusion.2 = (bf16[1280,512]{1,0:T(8,128)(2,1)S(1)}, f32[1280,512]{1,0:T(8,128)}) fusion(f32[1280,512]{1,0:T(8,128)S(1)} %copy-done.9, f32[1280,512]{1,0:T(8,128)S(1)} %fusion.19, bf16[1280,512]{1,0:T(8,128)(2,1)} %collective-permute-done, bf16[1536,512]{1,0:T(8,128)(2,1)} %param.21), kind=kOutput, calls=%fused_computation.22 | convolution fusion | flops 675676160 | bytes 11010048 | tf_op jit(solution)/shard_map/dot_general | solution.py:15
  41.7 1.9 multiply_add_fusion
  43.6 3.3 copy.28
  47.0 11.1 %scatter_custom_fusion = f32[320,512]{1,0:T(8,128)} fusion(s32[1280]{0:T(1024)S(1)} %copy-done.28, f32[1280,512]{1,0:T(8,128)} %copy.28, f32[]{:T(128)} %constant.10.clone.1), kind=kCustom, calls=%fused_computation.70 | custom fusion | flops 655360 | bytes 655872 | tf_op jit(solution)/shard_map/scatter-add | solution.py:141
  58.1 2.4 copy.27
  60.6 2.0 fusion.11
  62.6 5.1 %reduce-scatter.3.cloned.1.call-done = f32[160,512]{1,0:T(8,128)} async-done(((f32[320,512]{1,0:T(8,128)}), f32[160,512]{1,0:T(8,128)}) %reduce-scatter.3.cloned.1.call-update) | async-done | bytes 327696 | tf_op jit(solution)/shard_map/reduce_scatter | solution.py:142
  72.8 2.2 all_gather.7
  75.0 4.7 %gather_fusion.3 = bf16[1280,512]{1,0:T(8,128)(2,1)} fusion(bf16[320,512]{1,0:T(8,128)(2,1)S(1)} %all_gather.7, s32[2048]{0:T(1024)S(1)} %pad_clamp_fusion), kind=kCustom, calls=%fused_computation.3 | custom fusion | bytes 2626560 | tf_op jit(solution)/shard_map/gather | solution.py:147
  79.7 2.4 copy.29
  82.2 2.7 fusion.4
  90.8 1.9 fusion.51
  96.4 2.2 convolution_bitcast_fusion
  98.6 2.1 pad_maximum_fusion
  100.7 3.4 fusion.17
  104.2 11.4 %scatter_custom_fusion.1 = f32[448,512]{1,0:T(8,128)} fusion(s32[1280]{0:T(1024)S(1)} %copy-done.30, f32[1280,512]{1,0:T(8,128)} %fusion.17, f32[]{:T(128)} %constant.10.clone.1), kind=kCustom, calls=%fused_computation.55 | custom fusion | flops 655360 | bytes 918016 | tf_op jit(solution)/shard_map/scatter-add | solution.py:161
  116.7 1.6 fusion.37
  118.4 6.7 %all-to-all-start.1 = ((bf16[16,8,512]{2,1,0:T(8,128)(2,1)}), bf16[16,8,512]{2,1,0:T(8,128)(2,1)S(1)}, u32[]{:S(2)}, u32[]{:S(2)}) async-start(bf16[16,8,512]{2,1,0:T(8,128)(2,1)} %fusion.37), calls=%async_computation.2 | async-start | bytes 262144 | tf_op jit(solution)/shard_map/all_to_all | solution.py:166
  125.2 3.5 fusion.13
  128.6 10.6 %scatter_fusion = f32[320,512]{1,0:T(8,128)S(1)} fusion(f32[320,512]{1,0:T(8,128)S(1)} %slice.42, s32[1280]{0:T(1024)S(1)} %copy-done.28, f32[1280,512]{1,0:T(8,128)} %fusion.13), kind=kCustom, calls=%fused_computation.6 | custom fusion | flops 655360 | bytes 7869440 | tf_op jit(solution)/shard_map/scatter-add | solution.py:162
  143.2 3.0 fusion.1
  146.1 2.5 copy.32
  148.7 2.6 reduce-scatter.5.cloned.1.call-done
  151.3 2.0 fusion.7
  153.2 237.9 %all-reduce.5.cloned.1.call-done = (f32[1536,512]{1,0:T(8,128)}, f32[512,512]{1,0:T(8,128)}, f32[1024,512]{1,0:T(8,128)}, f32[512,512]{1,0:T(8,128)}) async-done(((f32[1536,512]{1,0:T(8,128)}, f32[512,512]{1,0:T(8,128)}, f32[1024,512]{1,0:T(8,128)}, f32[512,512]{1,0:T(8,128)}), (f32[1536,512]{1,0:T(8,128)}, f32[512,512]{1,0:T(8,128)}, f32[1024,512]{1,0:T(8,128)}, ...) | async-done | bytes 7340048 | tf_op jit(solution)/shard_map/psum | solution.py:178
  391.1 3.6 multiply_convert_fusion
  (123 shorter events, 28.0 us)
Async XLA Ops:
  7.2 32.8 %copy-start = (bf16[512,512]{1,0:T(8,128)(2,1)S(1)}, bf16[512,512]{1,0:T(8,128)(2,1)}, u32[]{:S(2)}) copy-start(bf16[512,512]{1,0:T(8,128)(2,1)} %param.22) | copy-start | bytes 1572868
  12.1 17.0 %all-to-all-start = ((bf16[16,8,512]{2,1,0:T(8,128)(2,1)}), bf16[16,8,512]{2,1,0:T(8,128)(2,1)S(1)}, u32[]{:S(2)}, u32[]{:S(2)}) async-start(bf16[16,8,512]{2,1,0:T(8,128)(2,1)} %bitcast.1), calls=%async_computation | async-start | bytes 262144 | tf_op jit(solution)/shard_map/all_to_all | solution.py:132
  20.3 47.4 %reduce-scatter.3.cloned.1.call-start = ((), (), s32[]{:S(2)}) async-start(), calls=%async_computation.4 | async-start | bytes 983040 | tf_op jit(solution)/shard_map/reduce_scatter | solution.py:142
  20.3 15.3 %collective-permute-start = (bf16[1280,512]{1,0:T(8,128)(2,1)}, bf16[1280,512]{1,0:T(8,128)(2,1)}, u32[]{:S(2)}, u32[]{:S(2)}) collective-permute-start(bf16[1280,512]{1,0:T(8,128)(2,1)} %param.15), channel_id=1, source_target_pairs={{0,1},{1,0},{2,3},{3,2},{4,5},{5,4},{6,7},{7,6},{8,9},{9,8},{10,11... | collective-permute-start | bytes 3932168 | tf_op jit(solution)/shard_map/ppermute | solution.py:11
  21.1 4.1 %copy-start.30 = (s32[1280]{0:T(1024)S(1)}, s32[1280]{0:T(1024)}, u32[]{:S(2)}) copy-start(s32[1280]{0:T(1024)} %param.18) | copy-start | bytes 15364
  25.3 3.8 copy-start.5
  33.2 2.4 copy-start.7
  33.2 2.4 copy-start.9
  43.6 3.3 copy-start.28
  47.0 13.6 %copy-start.13 = (bf16[160,512]{1,0:T(8,128)(2,1)S(1)}, bf16[160,512]{1,0:T(8,128)(2,1)}, u32[]{:S(2)}) copy-start(bf16[160,512]{1,0:T(8,128)(2,1)} %param.14) | copy-start | bytes 491524
  58.1 83.8 %all-reduce.7.cloned.1.call-start = ((), (), s32[]{:S(2)}) async-start(), calls=%async_computation.7 | async-start | bytes 14680064 | tf_op jit(solution)/shard_map/psum | solution.py:179
  62.6 8.4 %copy-start.24 = (bf16[160,512]{1,0:T(8,128)(2,1)S(1)}, bf16[160,512]{1,0:T(8,128)(2,1)}, u32[]{:S(2)}) copy-start(bf16[160,512]{1,0:T(8,128)(2,1)} %param.16) | copy-start | bytes 491524
  62.6 8.4 %copy-start.32 = (f32[512]{0:T(512)S(1)}, f32[512]{0:T(512)}, u32[]{:S(2)}) copy-start(f32[512]{0:T(512)} %param.27) | copy-start | bytes 6148
  67.7 3.6 copy-start.33
  69.2 2.4 copy-start.26
  82.2 2.7 copy-start.2
  82.2 2.7 copy-start.4
  84.9 1.7 copy-start.34
  90.8 1.9 copy-start.14
  90.8 1.9 copy-start.16
  90.8 2.3 copy-start.18
  90.8 2.3 copy-start.25
  90.8 2.3 copy-start.27
  92.7 1.8 copy-start.21
  118.4 20.9 %all-to-all-start.1 = ((bf16[16,8,512]{2,1,0:T(8,128)(2,1)}), bf16[16,8,512]{2,1,0:T(8,128)(2,1)S(1)}, u32[]{:S(2)}, u32[]{:S(2)}) async-start(bf16[16,8,512]{2,1,0:T(8,128)(2,1)} %fusion.37), calls=%async_computation.2 | async-start | bytes 262144 | tf_op jit(solution)/shard_map/all_to_all | solution.py:166
  125.1 26.1 %reduce-scatter.5.cloned.1.call-start = ((), (), s32[]{:S(2)}) async-start(), calls=%async_computation.5 | async-start | bytes 983040 | tf_op jit(solution)/shard_map/reduce_scatter | solution.py:172
  141.8 249.4 %all-reduce.5.cloned.1.call-start = ((), (), s32[]{:S(2)}) async-start(), calls=%async_computation.6 | async-start | bytes 14680064 | tf_op jit(solution)/shard_map/psum | solution.py:178
  146.1 5.1 %copy-start.11 = (bf16[1024,512]{1,0:T(8,128)(2,1)S(1)}, bf16[1024,512]{1,0:T(8,128)(2,1)}, u32[]{:S(2)}) copy-start(bf16[1024,512]{1,0:T(8,128)(2,1)} %param.25) | copy-start | bytes 3145732
  391.1 3.6 copy-start.23
  391.1 4.6 %copy-start.12 = (f32[1024,512]{1,0:T(8,128)S(1)}, f32[1024,512]{1,0:T(8,128)}, u32[]{:S(2)}) copy-start(f32[1024,512]{1,0:T(8,128)} %get-tuple-element.24) | copy-start | bytes 6291460
  394.7 2.2 copy-start.22
  395.7 2.2 copy-start.1
  (10 other events, 11.6 us)
Sparse Core Ops, SparseCore 0:
  58.2 9.4 reduce-scatter.2
  100.8 35.5 all-reduce.6
  141.9 9.3 reduce-scatter.4
  157.5 233.5 all-reduce.4
